TPU v7x, 256 devices: a whole 4x4x8 slice. The times are simulated.
256 devices in a mesh: dp: 32 (over x, y, core), expert: 8 (over z).
Axes of the slice: x: 4, y: 4, z: 8, core: 2. Of those that a mesh axis runs over, the one named last changes fastest.
Arguments:
- expert_master: float32 [8, 7168, 2048], P('expert', 'dp'), may hold values from -6 to 6
- expert_first: bfloat16 [8, 7168, 2048], P('expert', 'dp'), may hold values from -0.29882812 to 0.29882812
- expert_second: bfloat16 [8, 7168, 2048], P('expert', 'dp'), may hold values from 9.9658966e-05 to 0.0099487305
- expert_grad: bfloat16 [8, 7168, 2048], P('expert', 'dp'), may hold values from -0.29882812 to 0.29882812
- latent_master: float32 [7168, 1536], P(('dp', 'expert')), may hold values from -6 to 6
- latent_first: bfloat16 [7168, 1536], P(('dp', 'expert')), may hold values from -0.29882812 to 0.29882812
- latent_second: bfloat16 [7168, 1536], P(('dp', 'expert')), may hold values from 9.9658966e-05 to 0.0099487305
- latent_grad: bfloat16 [7168, 1536], P(('dp', 'expert')), may hold values from -0.29882812 to 0.29882812
- step_count: int32 [1], replicated, may hold values from 1 to 11
- column_owner: int32 [16], replicated, may hold values from 0 to 15, each once
Outputs:
- expert_master_new: float32 [8, 7168, 2048], P('expert', 'dp')
- expert_first_new: bfloat16 [8, 7168, 2048], P('expert', 'dp')
- expert_second_new: bfloat16 [8, 7168, 2048], P('expert', 'dp')
- expert_served: bfloat16 [8, 114688, 128], P('expert', 'dp')
- expert_scales: float32 [8, 896], P('expert', 'dp')
- latent_master_new: float32 [7168, 1536], P(('dp', 'expert'))
- latent_first_new: bfloat16 [7168, 1536], P(('dp', 'expert'))
- latent_second_new: bfloat16 [7168, 1536], P(('dp', 'expert'))
- latent_served: bfloat16 [7168, 1536], P('dp')
- latent_scales: float32 [56, 12], replicated
Inputs may be any that keep to these rules, and one draw needn't show every extreme that they name: column_owner names each serving position of the 16 column blocks exactly once.
All inputs are finite; a program needn't handle non-finite values. Where the computation divides by a largest or mean magnitude, that divisor is 1e-20 or more.
Results may differ from a plain program's by a relative error of at most 0.0017.
Values may be sent and summed in bfloat16 or wider, within the bound.
A program may use at most 64 MiB of HBM per device.

v0:
```python
import jax
import jax.numpy as jnp
from jax import lax
from jax.sharding import Mesh
from jax.sharding import PartitionSpec as P

D = 7168
TILE = 128
DP = ("dp_0", "dp_1", "dp_2")
DP_EXPERT = ("dp_0", "dp_1", "dp_2", "expert")


BETA_ONE = 0.9
BETA_TWO = 0.95
LEARN_RATE = 0.2
DECAY_RATE = 0.1
ADAM_EPS = 1e-08
SCALE_EPS = 1e-06


def by_axis(array, axes):
    for axis in axes:
        array = lax.pmax(array, axis)
    return array


def from_everyone(array, axis):
    devices = lax.axis_size(axis)
    return lax.all_to_all(
        jnp.broadcast_to(array[None], (devices, *array.shape)), axis, 0, 0, tiled=True
    )


def in_order(tiles, dim):
    tiles = jnp.moveaxis(tiles, 0, dim)
    lengths = tiles.shape
    return tiles.reshape(*lengths[:dim], lengths[dim] * lengths[dim + 1], *lengths[dim + 2 :])


def collect(array, axis, dim):
    tiles = from_everyone(array, axis)
    return in_order(tiles, dim)


def adamw_step(master, moment_one, moment_two, gradient, step_count):
    grad_value = gradient.astype(jnp.float32)
    first_new = BETA_ONE * moment_one.astype(jnp.float32) + (1.0 - BETA_ONE) * grad_value
    second_new = (
        BETA_TWO * moment_two.astype(jnp.float32) + (1.0 - BETA_TWO) * grad_value * grad_value
    )
    step_value = step_count[0].astype(jnp.float32)
    corr_one = 1.0 - jnp.power(jnp.float32(BETA_ONE), step_value)
    corr_two = 1.0 - jnp.power(jnp.float32(BETA_TWO), step_value)
    update = first_new / corr_one / (jnp.sqrt(second_new / corr_two) + ADAM_EPS)
    master_new = master - LEARN_RATE * (update + DECAY_RATE * master)
    return (master_new, first_new.astype(jnp.bfloat16), second_new.astype(jnp.bfloat16))


def row_maxima(weights):
    leading = weights.shape[:-1]
    tile_count = weights.shape[-1] // TILE
    return jnp.max(jnp.abs(weights).reshape(leading + (tile_count, TILE)), axis=-1)


def local_tiles(row_max, lead_rows):
    exp_count, row_count, tile_count = row_max.shape
    tile_span = row_count // TILE + 2
    buffer = jnp.zeros((exp_count, tile_span * TILE, tile_count), jnp.float32)
    buffer = lax.dynamic_update_slice(buffer, row_max, (jnp.int32(0), lead_rows, jnp.int32(0)))
    return jnp.max(buffer.reshape(exp_count, tile_span, TILE, tile_count), axis=2)


def place_tiles(tile_max, first_tile):
    exp_count, tile_span, tile_count = tile_max.shape
    global_map = jnp.zeros((exp_count, D // TILE + tile_span, tile_count), jnp.float32)
    return lax.dynamic_update_slice(global_map, tile_max, (jnp.int32(0), first_tile, jnp.int32(0)))


def quantized_rows(weights, tile_max, lead_rows):
    exp_count, row_count, col_count = weights.shape
    repeated = jnp.repeat(tile_max, TILE, axis=1)
    row_scale = lax.dynamic_slice_in_dim(repeated, lead_rows, row_count, 1)
    blocks = weights.reshape(exp_count, row_count, col_count // TILE, TILE)
    return (blocks / (row_scale[..., None] + SCALE_EPS)).reshape(weights.shape).astype(jnp.bfloat16)


def body(
    expert_master,
    expert_first,
    expert_second,
    expert_grad,
    latent_master,
    latent_first,
    latent_second,
    latent_grad,
    step_count,
    column_owner,
):
    master_new, first_new, second_new = adamw_step(
        expert_master, expert_first, expert_second, expert_grad, step_count
    )
    latent_new, latent_one, latent_two = adamw_step(
        latent_master, latent_first, latent_second, latent_grad, step_count
    )
    dp_count = lax.axis_size(DP)
    dp_pos = lax.axis_index(DP)
    exp_count, row_count, col_count = master_new.shape
    block_count = col_count // TILE
    slot_count = max(1, block_count // dp_count)
    total_tiles = D // TILE
    recv_rows = block_count * row_count
    recv_tiles = recv_rows // TILE
    positions = jnp.arange(block_count, dtype=jnp.int32)
    inverse = jnp.sum(
        positions[:, None] * (column_owner[:, None] == positions[None, :]).astype(jnp.int32), axis=0
    )
    receiver_ids = jnp.arange(dp_count, dtype=jnp.int32)[:, None]
    slot_ids = jnp.arange(slot_count, dtype=jnp.int32)[None, :]
    segment = (
        receiver_ids * block_count
        + jnp.mod(dp_pos - receiver_ids * block_count, dp_count)
        + slot_ids * dp_count
    )
    usable_slot = (segment < (receiver_ids + 1) * block_count).reshape(-1)
    send_block = jnp.take(inverse, jnp.minimum(segment // dp_count, block_count - 1)).reshape(-1)
    local_segments = jnp.arange(block_count, dtype=jnp.int32)
    source_dev = jnp.mod(dp_pos * block_count + local_segments, dp_count)
    pick_index = source_dev * slot_count + local_segments // dp_count
    blocks = master_new.reshape(exp_count, row_count, block_count, TILE)
    picked = jnp.take(blocks, send_block, axis=2)
    received = lax.all_to_all(
        jnp.where(usable_slot[None, None, :, None], picked, jnp.zeros((), picked.dtype)),
        DP,
        split_axis=2,
        concat_axis=2,
        tiled=True,
    )
    ordered = jnp.take(received, pick_index, axis=2)
    tall = (
        jnp.transpose(ordered, (0, 2, 1, 3))
        .reshape(exp_count, recv_rows, TILE)
        .reshape(exp_count, recv_tiles, TILE, TILE)
    )
    expert_scales = jnp.max(jnp.abs(tall), axis=(2, 3))
    expert_served = (
        (tall / (expert_scales[:, :, None, None] + SCALE_EPS))
        .reshape(exp_count, recv_rows, TILE)
        .astype(jnp.bfloat16)
    )
    latent_count = latent_new.shape[0]
    latent_offset = lax.axis_index(DP_EXPERT) * latent_count
    latent_lead = latent_offset % TILE
    latent_tiles = local_tiles(row_maxima(latent_new)[None], latent_lead)
    latent_map = by_axis(place_tiles(latent_tiles, latent_offset // TILE), DP_EXPERT)
    latent_scales = latent_map[0, :total_tiles]
    latent_tiles = lax.dynamic_slice_in_dim(
        latent_map, latent_offset // TILE, latent_tiles.shape[1], 1
    )
    latent_scaled = quantized_rows(latent_new[None], latent_tiles, latent_lead)[0]
    latent_served = collect(latent_scaled, "expert", 0)
    return (
        master_new,
        first_new,
        second_new,
        expert_served,
        expert_scales,
        latent_new,
        latent_one,
        latent_two,
        latent_served,
        latent_scales,
    )


def solution(mesh):
    torus = Mesh(
        mesh.devices.reshape(4, 4, 2, mesh.shape["expert"]), ("dp_0", "dp_1", "dp_2", "expert")
    )
    return jax.shard_map(
        body,
        mesh=torus,
        in_specs=(
            P("expert", DP, None),
            P("expert", DP, None),
            P("expert", DP, None),
            P("expert", DP, None),
            P(DP_EXPERT, None),
            P(DP_EXPERT, None),
            P(DP_EXPERT, None),
            P(DP_EXPERT, None),
            P(),
            P(),
        ),
        out_specs=(
            P("expert", DP, None),
            P("expert", DP, None),
            P("expert", DP, None),
            P("expert", DP, None),
            P("expert", DP),
            P(DP_EXPERT, None),
            P(DP_EXPERT, None),
            P(DP_EXPERT, None),
            P(DP, None),
            P(),
        ),
        check_vma=False,
    )
```

profile of v0, /device:TPU:1, one launch (start us, length us, event | category | flops | bytes accessed | tf_op | source)
XLA Modules:
  0.0 133.2 jit_solution(13130262668795441077)
XLA Ops:
  1.4 1.9 %fusion.25 = (f32[28,1536]{1,0:T(8,128)S(1)}, f32[28,1536]{1,0:T(8,128)S(1)}, bf16[28,1536]{1,0:T(8,128)(2,1)}, bf16[28,1536]{1,0:T(8,128)(2,1)}) fusion(f32[28,1536]{1,0:T(8,128)} %param.14, f32[]{:T(128)} %bitcast.1, bf16[28,1536]{1,0:T(8,128)(2,1)} %param.16, f32[]{:T(128)} %bitcast, bf16[28,1536]{1,0:T(8,128)(2,1)} %param.17, bf16[28,1536]{1,0:T(8,128)(2,1)} %param.15), kind=kLoop, calls=%fused_computation.96 | loop fusion | flops 903168 | bytes 946184 | tf_op jit(solution)/shard_map/abs | solution.py:62
  3.3 0.0 copy-start.3
  3.4 0.1 reduce_max.42
  3.5 0.1 copy.43
  3.6 0.3 dynamic_update_slice.6
  3.9 0.1 reduce_max.43
  4.0 0.3 dynamic_update_slice.7
  4.3 9.4 %pmax.28 = f32[1,58,12]{1,2,0:T(8,128)S(1)} all-reduce(f32[1,58,12]{1,2,0:T(8,128)S(1)} %dynamic_update_slice.7), channel_id=1, replica_groups=mesh['dp_0'=4,'dp_1'=4,'dp_2'=2,'expert'=8] {'dp_0'}, use_global_device_ids=true, to_apply=%region_5.6 | all-reduce | flops 696 | bytes 5568 | tf_op jit(solution)/shard_map/pmax | solution.py:23
  13.7 9.0 %pmax.29 = f32[1,58,12]{1,2,0:T(8,128)S(1)} all-reduce(f32[1,58,12]{1,2,0:T(8,128)S(1)} %pmax.28), channel_id=1, replica_groups=mesh['dp_0'=4,'dp_1'=4,'dp_2'=2,'expert'=8] {'dp_1'}, use_global_device_ids=true, to_apply=%region_6.7 | all-reduce | flops 696 | bytes 5568 | tf_op jit(solution)/shard_map/pmax | solution.py:23
  22.7 6.7 %pmax.30 = f32[1,58,12]{1,2,0:T(8,128)S(1)} all-reduce(f32[1,58,12]{1,2,0:T(8,128)S(1)} %pmax.29), channel_id=1, replica_groups=mesh['dp_0'=4,'dp_1'=4,'dp_2'=2,'expert'=8] {'dp_2'}, use_global_device_ids=true, to_apply=%region_7.8 | all-reduce | flops 696 | bytes 5568 | tf_op jit(solution)/shard_map/pmax | solution.py:23
  29.4 16.5 %pmax.31 = f32[1,58,12]{1,2,0:T(8,128)S(1)} all-reduce(f32[1,58,12]{1,2,0:T(8,128)S(1)} %pmax.30), channel_id=1, replica_groups=mesh['dp_0'=4,'dp_1'=4,'dp_2'=2,'expert'=8] {'expert'}, use_global_device_ids=true, to_apply=%region_8.9 | all-reduce | flops 696 | bytes 5568 | tf_op jit(solution)/shard_map/pmax | solution.py:23
  45.9 0.1 constant_dynamic-slice_fusion
  46.0 0.1 copy.46
  46.1 0.1 div.141
  46.2 0.0 copy-start.1
  46.2 0.0 copy-start.2
  46.3 0.1 copy.49
  46.4 0.9 broadcast_in_dim.78
  47.3 0.0 copy-done.3
  47.3 3.7 %all-to-all-start.1 = ((bf16[8,28,1536]{2,1,0:T(8,128)(2,1)}), bf16[8,28,1536]{2,1,0:T(8,128)(2,1)S(1)}, u32[]{:S(2)}, u32[]{:S(2)}) async-start(bf16[8,28,1536]{2,1,0:T(8,128)(2,1)} %broadcast_in_dim.78), calls=%async_computation.1 | async-start | bytes 1572864 | tf_op jit(solution)/shard_map/all_to_all | solution.py:29
  51.0 0.0 copy-done.1
  51.0 0.0 copy-done.2
  51.1 4.3 %fusion.7 = (bf16[1,224,2048]{2,1,0:T(8,128)(2,1)}, f32[1,224,2048]{2,1,0:T(8,128)S(1)}, bf16[1,224,2048]{2,1,0:T(8,128)(2,1)}) fusion(bf16[1,224,2048]{2,1,0:T(8,128)(2,1)S(1)} %copy-done.2, bf16[1,224,2048]{2,1,0:T(8,128)(2,1)} %param.12, f32[1,224,2048]{2,1,0:T(8,128)S(1)} %copy-done.1, f32[]{:T(128)} %bitcast.1, f32[]{:T(128)} %bitcast, ...), kind=kLoop, calls=%fused_computation.17 | loop fusion | flops 9175040 | bytes 8257544 | tf_op jit(solution)/shard_map/convert_element_type | solution.py:56
  55.3 0.0 copy-start
  55.4 0.3 copy.48
  55.7 0.9 copy-done
  56.6 0.0 copy-start.5
  56.6 0.6 copy.41
  57.2 0.0 copy-done.5
  57.2 0.1 select_reduce_fusion
  57.3 0.7 gather_fusion
  58.1 2.6 %gather_fusion.1 = f32[32,224,128]{2,1,0:T(8,128)} fusion(f32[224,16,128]{2,0,1:T(8,128)S(1)} %copy.41, s32[1024]{0:T(1024)S(1)} %pad_clamp_fusion.1), kind=kCustom, calls=%fused_computation.1 | custom fusion | bytes 7340160 | tf_op jit(solution)/shard_map/jit(_take)/gather | solution.py:130
  60.7 4.6 %fusion.1 = f32[1,224,32,128]{3,1,0,2:T(8,128)} fusion(f32[32,224,128]{2,1,0:T(8,128)} %gather_fusion.1, pred[32]{0:T(512)(128)(4,1)S(1)} %get-tuple-element.19, pred[32]{0:T(512)(128)(4,1)S(1)} %get-tuple-element.20), kind=kLoop, calls=%fused_computation.5 | loop fusion | flops 1835008 | bytes 7340096 | tf_op jit(solution)/shard_map/jit(_where)/select_n | solution.py:132
  65.3 5.9 %all-to-all-done.1 = bf16[8,28,1536]{2,1,0:T(8,128)(2,1)S(1)} async-done(((bf16[8,28,1536]{2,1,0:T(8,128)(2,1)}), bf16[8,28,1536]{2,1,0:T(8,128)(2,1)S(1)}, u32[]{:S(2)}, u32[]{:S(2)}) %all-to-all-start.1) | async-done | bytes 688160 | tf_op jit(solution)/shard_map/all_to_all | solution.py:29
  71.3 8.3 %all-to-all-start = ((f32[1,224,32,128]{3,1,0,2:T(8,128)}), f32[1,224,32,128]{3,1,0,2:T(8,128)}, u32[]{:S(2)}, u32[]{:S(2)}) async-start(f32[1,224,32,128]{3,1,0,2:T(8,128)} %fusion.1), calls=%async_computation | async-start | bytes 7340032 | tf_op jit(solution)/shard_map/all_to_all | solution.py:131
  79.6 0.6 slice_bitcast_fusion
  80.2 1.0 reshape.553
  81.2 44.2 %all-to-all-done = f32[1,224,32,128]{3,1,0,2:T(8,128)} async-done(((f32[1,224,32,128]{3,1,0,2:T(8,128)}), f32[1,224,32,128]{3,1,0,2:T(8,128)}, u32[]{:S(2)}, u32[]{:S(2)}) %all-to-all-start) | async-done | bytes 3670048 | tf_op jit(solution)/shard_map/all_to_all | solution.py:131
  125.3 4.0 %gather_fusion.2 = f32[16,224,128]{2,1,0:T(8,128)} fusion(f32[224,32,128]{2,0,1:T(8,128)} %bitcast.8, s32[1024]{0:T(1024)S(1)} %pad_clamp_fusion), kind=kCustom, calls=%fused_computation.2 | custom fusion | bytes 3670080 | tf_op jit(solution)/shard_map/jit(_take)/gather | solution.py:138
  129.3 2.2 %fusion.5 = (f32[16,224]{1,0:T(8,128)S(1)}, f32[1,224,16,128]{3,1,2,0:T(8,128)S(1)}) fusion(f32[16,224,128]{2,1,0:T(8,128)} %gather_fusion.2, pred[16]{0:T(512)(128)(4,1)S(1)} %compare_and_fusion.1), kind=kLoop, calls=%fused_computation.14 | loop fusion | flops 1372672 | bytes 3684368 | tf_op jit(solution)/shard_map/reduce_max | solution.py:144
  131.5 0.1 reduce_max.39
  131.6 0.1 reduce_max.40
  131.7 0.0 copy-start.4
  131.7 0.1 broadcast_bitcast_fusion
  131.8 1.5 %fusion.4 = bf16[1,3584,128]{2,1,0:T(8,128)(2,1)} fusion(f32[1,224,16,128]{3,1,2,0:T(8,128)S(1)} %get-tuple-element.13, f32[3584]{0:T(1024)S(1)} %broadcast_bitcast_fusion), kind=kLoop, calls=%fused_computation.11 | loop fusion | flops 917504 | bytes 2766848 | tf_op jit(solution)/shard_map/convert_element_type | solution.py:148
  133.2 0.0 copy-done.4
  (17 shorter events, 0.3 us)
Async XLA Ops:
  3.3 44.0 %copy-start.3 = (f32[28,1536]{1,0:T(8,128)}, f32[28,1536]{1,0:T(8,128)S(1)}, u32[]{:S(2)}) copy-start(f32[28,1536]{1,0:T(8,128)S(1)} %get-tuple-element.11) | copy-start | bytes 516100
  46.2 4.8 %copy-start.1 = (f32[1,224,2048]{2,1,0:T(8,128)S(1)}, f32[1,224,2048]{2,1,0:T(8,128)}, u32[]{:S(2)}) copy-start(f32[1,224,2048]{2,1,0:T(8,128)} %param.10) | copy-start | bytes 5505028
  46.2 4.8 %copy-start.2 = (bf16[1,224,2048]{2,1,0:T(8,128)(2,1)S(1)}, bf16[1,224,2048]{2,1,0:T(8,128)(2,1)}, u32[]{:S(2)}) copy-start(bf16[1,224,2048]{2,1,0:T(8,128)(2,1)} %param.13) | copy-start | bytes 2752516
  47.3 23.9 %all-to-all-start.1 = ((bf16[8,28,1536]{2,1,0:T(8,128)(2,1)}), bf16[8,28,1536]{2,1,0:T(8,128)(2,1)S(1)}, u32[]{:S(2)}, u32[]{:S(2)}) async-start(bf16[8,28,1536]{2,1,0:T(8,128)(2,1)} %broadcast_in_dim.78), calls=%async_computation.1 | async-start | bytes 1572864 | tf_op jit(solution)/shard_map/all_to_all | solution.py:29
  55.3 1.2 copy-start
  56.6 0.7 copy-start.5
  71.3 54.1 %all-to-all-start = ((f32[1,224,32,128]{3,1,0,2:T(8,128)}), f32[1,224,32,128]{3,1,0,2:T(8,128)}, u32[]{:S(2)}, u32[]{:S(2)}) async-start(f32[1,224,32,128]{3,1,0,2:T(8,128)} %fusion.1), calls=%async_computation | async-start | bytes 7340032 | tf_op jit(solution)/shard_map/all_to_all | solution.py:131
  131.7 1.6 %copy-start.4 = (f32[28]{0:T(128)}, f32[28]{0:T(128)S(1)}, u32[]{:S(2)}) copy-start(f32[28]{0:T(128)S(1)} %reduce_max.40) | copy-start | bytes 340
where the time goes:
time: 134 us; the launch traced here: 133 us
  waiting for transfers between devices  50.1 us (37%)
  blocking collectives  41.6 us (31%)
  other arithmetic  15.1 us (11%)
  local copies, waits for them, and re-layouts  12.9 us (10%)
  starting transfers between devices  11.9 us (9%)
  between operations  1.63 us (1%)
    all_to_all x1, waiting for transfers between devices, body(): lax.all_to_all(jnp.where(usable_slot[None, None, :, None], picked, jnp.ze...  44.2 us
    pmax x4, blocking collectives, by_axis(): array = lax.pmax(array, axis)  41.6 us
    all_to_all x1, starting transfers between devices, body(): lax.all_to_all(jnp.where(usable_slot[None, None, :, None], picked, jnp.ze...  8.26 us
    all_to_all x1, waiting for transfers between devices, from_everyone(): lax.all_to_all(jnp.broadcast_to(array[None], (devices, *array.shape)), ax...  5.94 us
    select_n x1, other arithmetic, body(): jnp.where(usable_slot[None, None, :, None], picked, jnp.zeros((), picked....  4.63 us
    convert_element_type x1, other arithmetic, adamw_step(): second_new.astype(jnp.bfloat16)  4.29 us
    gather x1, local copies, waits for them, and re-layouts, body(): ordered = jnp.take(received, pick_index, axis=2)  3.95 us
    all_to_all x1, starting transfers between devices, from_everyone(): lax.all_to_all(jnp.broadcast_to(array[None], (devices, *array.shape)), ax...  3.68 us
  transfers between devices with their start and end apart: 2, of which 2 were waited for; matrix products, arithmetic and copies ran while one was open for 11% of the time, Pallas kernels for 0%

commit v1 on v0

v1 whole, which is shorter than its diff:
```python
import jax
import jax.numpy as jnp
from jax import lax
from jax.experimental import pallas as pl
from jax.experimental.pallas import tpu as pltpu
from jax.sharding import Mesh
from jax.sharding import PartitionSpec as P

MESH = pl.DeviceIdType.MESH
TILE = 128
DP = ("dp_0", "dp_1", "dp_2")
DP_EXPERT = ("dp_0", "dp_1", "dp_2", "expert")

BETA_ONE = 0.9
BETA_TWO = 0.95
LEARN_RATE = 0.2
DECAY_RATE = 0.1
ADAM_EPS = 1e-08
SCALE_EPS = 1e-06

ROWS = 224
COLS = 2048
BLOCKS = COLS // TILE
SUB = 32
LROWS = 28
LCOLS = 1536
LBLOCKS = LCOLS // TILE
HALF = LCOLS // 2
LANE0 = 32
LINKS = 17

f32 = jnp.float32
bf16 = jnp.bfloat16


def iota2(shape, dim):
    return lax.broadcasted_iota(jnp.int32, shape, dim)


def adamw(master, first, second, grad, num_scale, den_scale):
    g = grad.astype(f32)
    first_new = BETA_ONE * first.astype(f32) + (1.0 - BETA_ONE) * g
    second_new = BETA_TWO * second.astype(f32) + (1.0 - BETA_TWO) * g * g
    update = (first_new * num_scale) / (jnp.sqrt(second_new * den_scale) + ADAM_EPS)
    master_new = (1.0 - LEARN_RATE * DECAY_RATE) * master - update
    return master_new, first_new.astype(bf16), second_new.astype(bf16)


def fold_rows(value):
    rows = value.shape[0]
    out = value[0:8]
    for r in range(8, rows, 8):
        out = jnp.maximum(out, value[r : r + 8])
    return out


def lanes_of(rows_value, first_lane):
    spread = jnp.broadcast_to(rows_value, (16, TILE))
    hit = iota2((16, TILE), 1) == iota2((16, TILE), 0) + first_lane
    return jnp.max(jnp.where(hit, spread, 0.0), axis=0, keepdims=True)


def blocks_of(row, first_lane):
    spread = jnp.broadcast_to(row, (16, TILE))
    hit = iota2((16, TILE), 1) == iota2((16, TILE), 0) + first_lane
    return jnp.max(jnp.where(hit, spread, 0.0), axis=1, keepdims=True)


def step_kernel(
    owner,
    step_count,
    w_hbm,
    m_hbm,
    v_hbm,
    g_hbm,
    lw_hbm,
    lm_hbm,
    lv_hbm,
    lg_hbm,
    w_out,
    m_out,
    v_out,
    served,
    rows_all,
    lw_out,
    lm_out,
    lv_out,
    lat,
    w_in,
    m_in,
    v_in,
    g_in,
    lw_in,
    lm_in,
    lv_in,
    lg_in,
    w_blocks,
    send,
    own_fold,
    next_fold,
    prev_fold,
    own_scale,
    own_recip,
    next_recip,
    prev_recip,
    next_scale,
    lfold_a,
    lfold_b,
    lrecip_a,
    lrecip_b,
    lrow_out,
    lrow_in,
    edge_out,
    edge_in,
    rows_out,
    inverse,
    in_sem,
    bulk_send,
    bulk_recv,
    self_sem,
    lrow_send,
    lrow_recv,
    edge_send,
    edge_recv,
    rows_send,
    rows_recv,
    ring_send,
    ring_recv,
):
    x = lax.axis_index("dp_0")
    y = lax.axis_index("dp_1")
    c = lax.axis_index("dp_2")
    z = lax.axis_index("expert")
    dp = (x * 4 + y) * 2 + c
    inner = lax.rem(y, 2) * 2 + c
    quad = lax.div(y, 2) * 2
    half = lax.div(x, 2)
    slot = lax.rem(dp, 16)
    is_self = c == half

    def dp_device(target, target_z):
        return (lax.div(target, 8), lax.rem(lax.div(target, 2), 4), lax.rem(target, 2), target_z)

    def quad_device(place, target_z):
        return (x, quad + lax.div(place, 2), lax.rem(place, 2), target_z)

    def up(value, n):
        return lax.rem(value, n)

    inner_next = up(inner + 1, 4)
    inner_prev = up(inner + 3, 4)

    loads = []

    def load(src, dst):
        copy = pltpu.make_async_copy(src, dst, in_sem.at[len(loads)])
        copy.start()
        loads.append(copy)

    for src, dst in ((lw_hbm, lw_in), (lm_hbm, lm_in), (lv_hbm, lv_in), (lg_hbm, lg_in)):
        load(src, dst)
    slabs = [pl.multiple_of(up(inner + j, 7) * SUB, SUB) for j in range(4, 7)]
    local = pl.multiple_of(inner * SUB, SUB)
    pairs = ((w_hbm, w_in), (m_hbm, m_in), (v_hbm, v_in), (g_hbm, g_in))
    for src, dst in pairs:
        for s in slabs:
            load(src.at[pl.ds(s, SUB), :], dst.at[pl.ds(s, SUB), :])
    for src, dst in pairs:
        load(src.at[pl.ds(local, TILE), :], dst.at[pl.ds(local, TILE), :])

    barrier = pltpu.get_barrier_semaphore()

    def greet(device):
        pl.semaphore_signal(barrier, inc=1, device_id=device, device_id_type=MESH)

    @pl.loop(1, 8)
    def _(d):
        greet((x, y, c, up(z + d, 8)))

    @pl.loop(1, 6)
    def _(d):
        greet(quad_device(inner_next, up(z + d, 8)))

    @pl.loop(3, 8)
    def _(d):
        greet(quad_device(inner_prev, up(z + d, 8)))

    @pl.loop(1, 32)
    def _(d):
        greet(dp_device(up(dp + d, 32), z))

    @pl.loop(0, 16)
    def _(k):
        p = up(x + lax.div(k, 4), 4) * 4 + up(y + lax.rem(k, 4), 4)
        total = jnp.int32(0)
        for b in range(BLOCKS):
            total = jnp.maximum(total, jnp.where(owner[b] == p, b, 0))
        inverse[k] = total

    steps = jnp.full((8, TILE), step_count[0], jnp.int32).astype(f32)
    num_scale = (LEARN_RATE / (1.0 - jnp.power(jnp.full((8, TILE), BETA_ONE, f32), steps)))[0:1]
    den_scale = (1.0 / (1.0 - jnp.power(jnp.full((8, TILE), BETA_TWO, f32), steps)))[0:1]

    for copy in loads[:4]:
        copy.wait()
    lat_place = (inner * 8 + z) * LROWS
    lat_block = lax.div(lat_place, TILE)
    lat_edge = TILE - lax.rem(lat_place, TILE)
    lat_rows = iota2((LROWS, TILE), 0)

    for b in range(LBLOCKS):
        cols = pl.ds(b * TILE, TILE)
        w1, m1, v1 = adamw(
            lw_in[:, cols], lm_in[:, cols], lv_in[:, cols], lg_in[:, cols], num_scale, den_scale
        )
        lw_out[:, cols] = w1
        lm_out[:, cols] = m1
        lv_out[:, cols] = v1
        size = jnp.abs(w1)
        lfold_a[b : b + 1, :] = jnp.max(
            jnp.where(lat_rows < lat_edge, size, 0.0), axis=0, keepdims=True
        )
        lfold_b[b : b + 1, :] = jnp.max(
            jnp.where(lat_rows >= lat_edge, size, 0.0), axis=0, keepdims=True
        )
    real = iota2((16, 1), 0) < LBLOCKS
    first_lane = LANE0 + lat_block * LBLOCKS
    max_a = jnp.where(real, jnp.max(lfold_a[...], axis=1, keepdims=True), 0.0)
    max_b = jnp.where(real, jnp.max(lfold_b[...], axis=1, keepdims=True), 0.0)
    lrow = jnp.maximum(lanes_of(max_a, first_lane), lanes_of(max_b, first_lane + LBLOCKS))
    lrow_out[0] = lrow

    for copy in loads[4:16]:
        copy.wait()

    @pl.loop(0, BLOCKS)
    def _(b):
        cols = pl.ds(pl.multiple_of(b * TILE, TILE), TILE)
        after = jnp.zeros((8, TILE), f32)
        before = jnp.zeros((8, TILE), f32)
        for j, s in zip(range(4, 7), slabs):
            rows = pl.ds(s, SUB)
            w1, m1, v1 = adamw(
                w_in[rows, cols], m_in[rows, cols], v_in[rows, cols], g_in[rows, cols],
                num_scale, den_scale,
            )
            w_out[rows, cols] = w1
            w_blocks[b, rows, :] = w1
            m_out[rows, cols] = m1
            v_out[rows, cols] = v1
            size = fold_rows(jnp.abs(w1))
            is_after = inner + j < 7
            after = jnp.maximum(after, jnp.where(is_after, size, 0.0))
            before = jnp.maximum(before, jnp.where(is_after, 0.0, size))
        next_fold[b] = after
        prev_fold[b] = before

    def widest(fold):
        return jnp.max(jnp.max(fold[...], axis=1), axis=1, keepdims=True)

    edge_out[0] = lanes_of(widest(next_fold), 0)
    edge_out[1] = lanes_of(widest(prev_fold), 0)

    pl.semaphore_wait(barrier, LINKS + 31)

    def edge_copy(n, place):
        return pltpu.make_async_remote_copy(
            src_ref=edge_out.at[n],
            dst_ref=edge_in.at[n],
            send_sem=edge_send.at[n],
            recv_sem=edge_recv.at[n],
            device_id=quad_device(place, z),
            device_id_type=MESH,
        )

    edges = [edge_copy(0, inner_next), edge_copy(1, inner_prev)]
    for copy in edges:
        copy.start()

    def lrow_copy(n, device):
        return pltpu.make_async_remote_copy(
            src_ref=lrow_out.at[0],
            dst_ref=lrow_in.at[n],
            send_sem=lrow_send,
            recv_sem=lrow_recv,
            device_id=device,
            device_id_type=MESH,
        )

    @pl.loop(1, 8)
    def _(d):
        lrow_copy(d - 1, (x, y, c, up(z + d, 8))).start()

    @pl.loop(1, 6)
    def _(d):
        lrow_copy(d + 6, quad_device(inner_next, up(z + d, 8))).start()

    @pl.loop(3, 8)
    def _(d):
        lrow_copy(d + 9, quad_device(inner_prev, up(z + d, 8))).start()

    for copy in loads[16:]:
        copy.wait()
    own = pl.ds(local, TILE)

    @pl.loop(0, BLOCKS)
    def _(b):
        cols = pl.ds(pl.multiple_of(b * TILE, TILE), TILE)
        w1, m1, v1 = adamw(
            w_in[own, cols], m_in[own, cols], v_in[own, cols], g_in[own, cols], num_scale, den_scale
        )
        w_out[own, cols] = w1
        w_blocks[b, own, :] = w1
        m_out[own, cols] = m1
        v_out[own, cols] = v1
        own_fold[b] = fold_rows(jnp.abs(w1))

    def spread(scale):
        return jnp.broadcast_to(scale, (16, TILE))

    def recip(scale):
        return spread(1.0 / (scale + SCALE_EPS))

    def put(ref, value):
        for b in range(BLOCKS):
            ref[b] = value[b : b + 1]

    own_max = widest(own_fold)
    put(own_scale, spread(own_max))
    put(own_recip, recip(own_max))

    def target(k):
        return (up(x + lax.div(k, 4), 4), up(y + lax.rem(k, 4), 4), half, z)

    def bulk(k, rows, start):
        src = send.at[k, pl.ds(rows, start[1]), :]
        dst = served.at[slot, pl.ds(rows, start[1]), :]
        return src, dst

    def bulk_start(k, rows, count):
        src = send.at[k, pl.ds(rows, count), :]
        dst = served.at[slot, pl.ds(rows, count), :]
        stays = jnp.logical_and(is_self, k == 0)

        @pl.when(stays)
        def _():
            pltpu.make_async_copy(src, dst, self_sem).start()

        @pl.when(jnp.logical_not(stays))
        def _():
            pltpu.make_async_remote_copy(
                src_ref=src,
                dst_ref=dst,
                send_sem=bulk_send,
                recv_sem=bulk_recv,
                device_id=target(k),
                device_id_type=MESH,
            ).start()

    @pl.loop(0, 16)
    def _(k):
        b = inverse[k]
        send[k, own, :] = (w_blocks[b, own, :] * own_recip[b]).astype(bf16)

    @pl.loop(0, 16)
    def _(k):
        bulk_start(k, local, TILE)

    for copy in edges:
        copy.wait_recv()
    prev_max = blocks_of(jnp.maximum(edge_out[1], edge_in[0]), 0)
    next_max = blocks_of(jnp.maximum(edge_out[0], edge_in[1]), 0)
    put(prev_recip, recip(prev_max))
    put(next_recip, recip(next_max))
    put(next_scale, spread(next_max))

    @pl.loop(0, 16)
    def _(k):
        b = inverse[k]
        after = next_recip[b]
        before = prev_recip[b]
        for j, s in zip(range(4, 7), slabs):
            rows = pl.ds(s, SUB)
            scale = jnp.where(inner + j < 7, after, before)
            send[k, rows, :] = (w_blocks[b, rows, :] * scale).astype(bf16)

    pltpu.make_async_copy(lrow_in, lrow_in, lrow_recv).wait()
    lmax = jnp.maximum(lrow, jnp.max(lrow_in[...], axis=0))
    lrecip_a[...] = recip(blocks_of(lmax, first_lane))
    lrecip_b[...] = recip(blocks_of(lmax, first_lane + LBLOCKS))

    for b in range(LBLOCKS):
        cols = pl.ds(b * TILE, TILE)
        scale = jnp.where(lat_rows < lat_edge, lrecip_a[b : b + 1, :], lrecip_b[b : b + 1, :])
        lat[z, :, cols] = (lw_out[:, cols] * scale).astype(bf16)

    lane = iota2((1, TILE), 1)
    scale_lane = 7 * lax.div(slot, 4) + 2 * inner
    lat_lanes = jnp.where(lane >= LANE0, lmax, 0.0)

    def message(k):
        b = inverse[k]
        value = jnp.where(lane == scale_lane, own_scale[b], lat_lanes)
        both = jnp.logical_and(lane == scale_lane + 1, inner < 3)
        return jnp.where(both, next_scale[b], value)

    @pl.loop(0, 16)
    def _(k):
        rows_out[k] = message(k)

    def ring_copy(way, hop, part):
        origin = up(z + 8 - hop, 8) if way == 0 else up(z + hop, 8)
        peer = up(z + 1, 8) if way == 0 else up(z + 7, 8)
        view = lat.at[origin, :, pl.ds(part * HALF, HALF)]
        n = (way * 4 + hop) * 2 + part
        return pltpu.make_async_remote_copy(
            src_ref=view,
            dst_ref=view,
            send_sem=ring_send.at[n],
            recv_sem=ring_recv.at[n],
            device_id=(x, y, c, peer),
            device_id_type=MESH,
        )

    def arrived(way, hop, part):
        origin = up(z + 7 - hop, 8) if way == 0 else up(z + 1 + hop, 8)
        view = lat.at[origin, :, pl.ds(part * HALF, HALF)]
        n = (way * 4 + hop) * 2 + part
        pltpu.make_async_copy(view, view, ring_recv.at[n]).wait()

    hops = [
        (way, hop, part)
        for hop in range(4)
        for part in range(2)
        for way in range(2)
        if hop < 3 or part == way
    ]
    sent = []
    for way, hop, part in hops:
        if hop == 0:
            copy = ring_copy(way, hop, part)
            copy.start()
            sent.append(copy)

    def rows_copy(k, core):
        return pltpu.make_async_remote_copy(
            src_ref=rows_out.at[k],
            dst_ref=rows_all.at[dp],
            send_sem=rows_send,
            recv_sem=rows_recv,
            device_id=(up(x + lax.div(k, 4), 4), up(y + lax.rem(k, 4), 4), core, z),
            device_id_type=MESH,
        )

    rows_all[dp] = rows_out[0]
    rows_copy(0, 1 - c).start()

    @pl.loop(1, 16)
    def _(k):
        rows_copy(k, 0).start()
        rows_copy(k, 1).start()

    for j, s in zip(range(4, 7), slabs):

        @pl.loop(0, 16)
        def _(k):
            bulk_start(k, s, SUB)

    for way, hop, part in hops:
        arrived(way, hop, part)
        if (way, hop + 1, part) in hops:
            copy = ring_copy(way, hop + 1, part)
            copy.start()
            sent.append(copy)

    for copy in sent:
        copy.wait_send()
    for copy in edges:
        copy.wait_send()
    pltpu.make_async_copy(lrow_in, lrow_in, lrow_send).wait()
    few = rows_all.at[pl.ds(0, 31)]
    pltpu.make_async_copy(few, few, rows_send).wait()
    pltpu.make_async_copy(few, few, rows_recv).wait()

    @pl.when(is_self)
    def _():
        one = served.at[0]
        rest = served.at[pl.ds(0, 15)]
        pltpu.make_async_copy(one, one, self_sem).wait()
        pltpu.make_async_copy(rest, rest, bulk_send).wait()
        pltpu.make_async_copy(rest, rest, bulk_recv).wait()

    @pl.when(jnp.logical_not(is_self))
    def _():
        pltpu.make_async_copy(served, served, bulk_send).wait()
        pltpu.make_async_copy(served, served, bulk_recv).wait()


def store_kernel(
    w_in,
    m_in,
    v_in,
    served_in,
    rows_in,
    lw_in,
    lm_in,
    lv_in,
    lat_in,
    w_hbm,
    m_hbm,
    v_hbm,
    served_hbm,
    scales_hbm,
    lw_hbm,
    lm_hbm,
    lv_hbm,
    lserved_hbm,
    lscales_hbm,
    lserved,
    scales,
    lscales,
    lscales_tall,
    sem,
):
    copies = []

    def store(src, dst):
        copy = pltpu.make_async_copy(src, dst, sem.at[len(copies)])
        copy.start()
        copies.append(copy)

    for src, dst in (
        (w_in, w_hbm),
        (m_in, m_hbm),
        (v_in, v_hbm),
        (served_in, served_hbm),
        (lw_in, lw_hbm),
        (lm_in, lm_hbm),
        (lv_in, lv_hbm),
    ):
        store(src, dst)
    for o in range(8):
        lserved[o * LROWS : (o + 1) * LROWS, :] = lat_in[o]
    store(lserved, lserved_hbm)
    c = lax.axis_index("dp_2")
    mine = jnp.max(rows_in[pl.ds(c * 16, 16)], axis=0)
    scales[...] = mine[:, 0:28]
    for g in range(8):
        group = jnp.max(rows_in[4 * g : 4 * g + 4], axis=0)
        for r in range(7):
            lane = LANE0 + r * LBLOCKS
            lscales_tall[7 * g + r : 7 * g + r + 1, 0:LBLOCKS] = group[:, lane : lane + LBLOCKS]
    lscales[...] = lscales_tall[...].T[0:LBLOCKS, 0:56]
    store(scales, scales_hbm)
    store(lscales, lscales_hbm)
    for copy in copies:
        copy.wait()


def body(
    expert_master,
    expert_first,
    expert_second,
    expert_grad,
    latent_master,
    latent_first,
    latent_second,
    latent_grad,
    step_count,
    column_owner,
):
    smem = pl.BlockSpec(memory_space=pltpu.SMEM)
    hbm = pl.BlockSpec(memory_space=pltpu.HBM)
    vmem = pl.BlockSpec(memory_space=pltpu.VMEM)
    dma = pltpu.SemaphoreType.DMA
    row = (1, TILE)
    made = pl.pallas_call(
        step_kernel,
        out_shape=(
            pltpu.VMEM((ROWS, COLS), f32),
            pltpu.VMEM((ROWS, COLS), bf16),
            pltpu.VMEM((ROWS, COLS), bf16),
            pltpu.VMEM((16, ROWS, TILE), bf16),
            pltpu.VMEM((32, *row), f32),
            pltpu.VMEM((LROWS, LCOLS), f32),
            pltpu.VMEM((LROWS, LCOLS), bf16),
            pltpu.VMEM((LROWS, LCOLS), bf16),
            pltpu.VMEM((8, LROWS, LCOLS), bf16),
        ),
        in_specs=[smem, smem] + [hbm] * 8,
        out_specs=(vmem,) * 9,
        scratch_shapes=[
            pltpu.VMEM((ROWS, COLS), f32),
            pltpu.VMEM((ROWS, COLS), bf16),
            pltpu.VMEM((ROWS, COLS), bf16),
            pltpu.VMEM((ROWS, COLS), bf16),
            pltpu.VMEM((LROWS, LCOLS), f32),
            pltpu.VMEM((LROWS, LCOLS), bf16),
            pltpu.VMEM((LROWS, LCOLS), bf16),
            pltpu.VMEM((LROWS, LCOLS), bf16),
            pltpu.VMEM((16, ROWS, TILE), f32),
            pltpu.VMEM((16, ROWS, TILE), bf16),
            pltpu.VMEM((16, 8, TILE), f32),
            pltpu.VMEM((16, 8, TILE), f32),
            pltpu.VMEM((16, 8, TILE), f32),
            pltpu.VMEM((16, *row), f32),
            pltpu.VMEM((16, *row), f32),
            pltpu.VMEM((16, *row), f32),
            pltpu.VMEM((16, *row), f32),
            pltpu.VMEM((16, *row), f32),
            pltpu.VMEM((16, TILE), f32),
            pltpu.VMEM((16, TILE), f32),
            pltpu.VMEM((16, TILE), f32),
            pltpu.VMEM((16, TILE), f32),
            pltpu.VMEM((1, *row), f32),
            pltpu.VMEM((LINKS, *row), f32),
            pltpu.VMEM((2, *row), f32),
            pltpu.VMEM((2, *row), f32),
            pltpu.VMEM((16, *row), f32),
            pltpu.SMEM((16,), jnp.int32),
            dma((20,)),
            dma,
            dma,
            dma,
            dma,
            dma,
            dma((2,)),
            dma((2,)),
            dma,
            dma,
            dma((16,)),
            dma((16,)),
        ],
        compiler_params=pltpu.CompilerParams(
            collective_id=0, has_side_effects=True, vmem_limit_bytes=24 << 20
        ),
        name="step",
    )(
        column_owner,
        step_count,
        *(
            pltpu.with_memory_space_constraint(value, pltpu.HBM)
            for value in (
                expert_master[0],
                expert_first[0],
                expert_second[0],
                expert_grad[0],
                latent_master,
                latent_first,
                latent_second,
                latent_grad,
            )
        ),
    )
    out = pl.pallas_call(
        store_kernel,
        out_shape=(
            jax.ShapeDtypeStruct((ROWS, COLS), f32),
            jax.ShapeDtypeStruct((ROWS, COLS), bf16),
            jax.ShapeDtypeStruct((ROWS, COLS), bf16),
            jax.ShapeDtypeStruct((16, ROWS, TILE), bf16),
            jax.ShapeDtypeStruct((1, 28), f32),
            jax.ShapeDtypeStruct((LROWS, LCOLS), f32),
            jax.ShapeDtypeStruct((LROWS, LCOLS), bf16),
            jax.ShapeDtypeStruct((LROWS, LCOLS), bf16),
            jax.ShapeDtypeStruct((ROWS, LCOLS), bf16),
            jax.ShapeDtypeStruct((LBLOCKS, 56), f32),
        ),
        in_specs=[vmem] * 9,
        out_specs=(hbm,) * 10,
        scratch_shapes=[
            pltpu.VMEM((ROWS, LCOLS), bf16),
            pltpu.VMEM((1, 28), f32),
            pltpu.VMEM((LBLOCKS, 56), f32),
            pltpu.VMEM((TILE, TILE), f32),
            dma((10,)),
        ],
        compiler_params=pltpu.CompilerParams(vmem_limit_bytes=8 << 20),
        name="store",
    )(*made)
    master, first, second, served, scales, lmaster, lfirst, lsecond, lserved, lscales = out
    return (
        master[None],
        first[None],
        second[None],
        served.reshape(1, 16 * ROWS, TILE),
        scales,
        lmaster,
        lfirst,
        lsecond,
        lserved,
        lscales.T,
    )


def solution(mesh):
    torus = Mesh(
        mesh.devices.reshape(4, 4, 2, mesh.shape["expert"]), ("dp_0", "dp_1", "dp_2", "expert")
    )
    expert = P("expert", DP, None)
    latent = P(DP_EXPERT, None)
    return jax.shard_map(
        body,
        mesh=torus,
        in_specs=(expert,) * 4 + (latent,) * 4 + (P(), P()),
        out_specs=(
            expert,
            expert,
            expert,
            expert,
            P("expert", DP),
            latent,
            latent,
            latent,
            P(DP, None),
            P(),
        ),
        check_vma=False,
    )
```

time: 134 us -> 35 us (0.26)
  the two profiles are of different devices: /device:TPU:1 before, /device:TPU:8 now
where the time goes in v1:
time: 35 us; the launch traced here: 34.9 us
  Pallas kernels  32.9 us (94%)
  between operations  1.31 us (4%)
  local copies, waits for them, and re-layouts  0.65 us (2%)
    pallas_call x1, Pallas kernels, body(): pl.pallas_call(step_kernel, out_shape=(pltpu.VMEM((ROWS, COLS), f32), plt...  30.3 us
    pallas_call x1, Pallas kernels, body(): pl.pallas_call(store_kernel, out_shape=(jax.ShapeDtypeStruct((ROWS, COLS)...  2.64 us

profile of v1, /device:TPU:8, one launch (start us, length us, event | category | flops | bytes accessed | tf_op | source)
XLA Modules:
  0.0 34.9 jit_solution(14790479017111130540)
XLA Ops:
  1.3 0.0 copy-start
  1.3 0.6 %copy-done = s32[16]{0:T(128)S(1)} copy-done((s32[16]{0:T(128)S(1)}, s32[16]{0:T(128)}, u32[]{:S(2)}) %copy-start) | copy-done | bytes 88
  1.9 30.3 %step.1 = (f32[224,2048]{1,0:T(8,128)S(1)}, bf16[224,2048]{1,0:T(8,128)(2,1)S(1)}, bf16[224,2048]{1,0:T(8,128)(2,1)S(1)}, bf16[16,224,128]{2,1,0:T(8,128)(2,1)S(...) custom-call(s32[16]{0:T(128)S(1)} %copy-done, ...), custom_call_target="tpu_custom_call" | custom-call | tf_op jit(solution)/shard_map/step/pallas_call | solution.py:577
  32.2 2.6 %store.1 = (f32[224,2048]{1,0:T(8,128)}, bf16[224,2048]{1,0:T(8,128)(2,1)}, bf16[224,2048]{1,0:T(8,128)(2,1)}, bf16[16,224,128]{2,1,0:T(8,128)(2,1)}, f32[1,28]{...) custom-call(f32[224,2048]{1,0:T(8,128)S(1)} %get-tuple-element.29.w_, ...), custom_call_target="tpu_custom_call" | custom-call | tf_op jit(solution)/shard_map/store/pallas_call | solution.py:655
Async XLA Ops:
  1.3 0.7 %copy-start = (s32[16]{0:T(128)S(1)}, s32[16]{0:T(128)}, u32[]{:S(2)}) copy-start(s32[16]{0:T(128)} %owner.1) | copy-start | bytes 196

commit v2 on v1

--- a/solution.py
+++ b/solution.py
@@ -25,9 +25,11 @@
 LROWS = 28
 LCOLS = 1536
 LBLOCKS = LCOLS // TILE
-HALF = LCOLS // 2
+LFLAT = LROWS * LBLOCKS
+PARTS = 2
+PART = LFLAT // PARTS
 LANE0 = 32
-LINKS = 17
+GROUP = 32
 
 f32 = jnp.float32
 bf16 = jnp.bfloat16
@@ -67,8 +69,8 @@
 
 
 def step_kernel(
-    owner,
     step_count,
+    owner_hbm,
     w_hbm,
     m_hbm,
     v_hbm,
@@ -106,22 +108,25 @@
     next_scale,
     lfold_a,
     lfold_b,
-    lrecip_a,
-    lrecip_b,
     lrow_out,
     lrow_in,
     edge_out,
     edge_in,
     rows_out,
+    lflat,
+    lscaled,
+    lnear,
+    owner,
     inverse,
     in_sem,
     bulk_send,
     bulk_recv,
-    self_sem,
     lrow_send,
     lrow_recv,
     edge_send,
     edge_recv,
+    near_send,
+    near_recv,
     rows_send,
     rows_recv,
     ring_send,
@@ -147,6 +152,12 @@
     def up(value, n):
         return lax.rem(value, n)
 
+    place = inner * 8 + z
+
+    def group_device(d):
+        other = up(place + d, GROUP)
+        return quad_device(lax.div(other, 8), up(other, 8))
+
     inner_next = up(inner + 1, 4)
     inner_prev = up(inner + 3, 4)
 
@@ -163,31 +174,64 @@
     local = pl.multiple_of(inner * SUB, SUB)
     pairs = ((w_hbm, w_in), (m_hbm, m_in), (v_hbm, v_in), (g_hbm, g_in))
     for src, dst in pairs:
+        load(src.at[pl.ds(local, TILE), :], dst.at[pl.ds(local, TILE), :])
+    for src, dst in pairs:
         for s in slabs:
             load(src.at[pl.ds(s, SUB), :], dst.at[pl.ds(s, SUB), :])
-    for src, dst in pairs:
-        load(src.at[pl.ds(local, TILE), :], dst.at[pl.ds(local, TILE), :])
+
+    load(owner_hbm, owner)
 
     barrier = pltpu.get_barrier_semaphore()
 
     def greet(device):
         pl.semaphore_signal(barrier, inc=1, device_id=device, device_id_type=MESH)
 
-    @pl.loop(1, 8)
+    @pl.loop(1, GROUP)
     def _(d):
-        greet((x, y, c, up(z + d, 8)))
-
-    @pl.loop(1, 6)
-    def _(d):
-        greet(quad_device(inner_next, up(z + d, 8)))
-
-    @pl.loop(3, 8)
-    def _(d):
-        greet(quad_device(inner_prev, up(z + d, 8)))
-
-    @pl.loop(1, 32)
-    def _(d):
-        greet(dp_device(up(dp + d, 32), z))
+        greet(group_device(d))
+        greet(dp_device(up(dp + d, GROUP), z))
+
+    steps = jnp.full((8, TILE), step_count[0], jnp.int32).astype(f32)
+    num_scale = (LEARN_RATE / (1.0 - jnp.power(jnp.full((8, TILE), BETA_ONE, f32), steps)))[0:1]
+    den_scale = (1.0 / (1.0 - jnp.power(jnp.full((8, TILE), BETA_TWO, f32), steps)))[0:1]
+
+    for copy in loads[:4]:
+        copy.wait()
+    lat_rows = iota2((LROWS, TILE), 0)
+
+    def lat_blocks(origin):
+        start = (inner * 8 + origin) * LROWS
+        return LANE0 + lax.div(start, TILE) * LBLOCKS, lat_rows < TILE - lax.rem(start, TILE)
+
+    first_lane, in_first = lat_blocks(z)
+
+    for b in range(LBLOCKS):
+        cols = pl.ds(b * TILE, TILE)
+        w1, m1, v1 = adamw(
+            lw_in[:, cols], lm_in[:, cols], lv_in[:, cols], lg_in[:, cols], num_scale, den_scale
+        )
+        lw_out[:, cols] = w1
+        lflat[b * LROWS : (b + 1) * LROWS, :] = w1
+        lm_out[:, cols] = m1
+        lv_out[:, cols] = v1
+        size = jnp.abs(w1)
+        lfold_a[b : b + 1, :] = jnp.max(
+            jnp.where(in_first, size, 0.0), axis=0, keepdims=True
+        )
+        lfold_b[b : b + 1, :] = jnp.max(
+            jnp.where(in_first, 0.0, size), axis=0, keepdims=True
+        )
+    real = iota2((16, 1), 0) < LBLOCKS
+    max_a = jnp.where(real, jnp.max(lfold_a[...], axis=1, keepdims=True), 0.0)
+    max_b = jnp.where(real, jnp.max(lfold_b[...], axis=1, keepdims=True), 0.0)
+    lrow = jnp.maximum(lanes_of(max_a, first_lane), lanes_of(max_b, first_lane + LBLOCKS))
+    lrow_out[0] = lrow
+    lrow_in[place] = lrow
+
+    def widest(fold):
+        return jnp.max(jnp.max(fold[...], axis=1), axis=1, keepdims=True)
+
+    loads[20].wait()
 
     @pl.loop(0, 16)
     def _(k):
@@ -197,40 +241,97 @@
             total = jnp.maximum(total, jnp.where(owner[b] == p, b, 0))
         inverse[k] = total
 
-    steps = jnp.full((8, TILE), step_count[0], jnp.int32).astype(f32)
-    num_scale = (LEARN_RATE / (1.0 - jnp.power(jnp.full((8, TILE), BETA_ONE, f32), steps)))[0:1]
-    den_scale = (1.0 / (1.0 - jnp.power(jnp.full((8, TILE), BETA_TWO, f32), steps)))[0:1]
-
-    for copy in loads[:4]:
+    for copy in loads[4:8]:
         copy.wait()
-    lat_place = (inner * 8 + z) * LROWS
-    lat_block = lax.div(lat_place, TILE)
-    lat_edge = TILE - lax.rem(lat_place, TILE)
-    lat_rows = iota2((LROWS, TILE), 0)
-
-    for b in range(LBLOCKS):
-        cols = pl.ds(b * TILE, TILE)
+    own = pl.ds(local, TILE)
+
+    @pl.loop(0, BLOCKS)
+    def _(b):
+        cols = pl.ds(pl.multiple_of(b * TILE, TILE), TILE)
         w1, m1, v1 = adamw(
-            lw_in[:, cols], lm_in[:, cols], lv_in[:, cols], lg_in[:, cols], num_scale, den_scale
+            w_in[own, cols], m_in[own, cols], v_in[own, cols], g_in[own, cols], num_scale, den_scale
         )
-        lw_out[:, cols] = w1
-        lm_out[:, cols] = m1
-        lv_out[:, cols] = v1
-        size = jnp.abs(w1)
-        lfold_a[b : b + 1, :] = jnp.max(
-            jnp.where(lat_rows < lat_edge, size, 0.0), axis=0, keepdims=True
+        w_out[own, cols] = w1
+        w_blocks[b, own, :] = w1
+        m_out[own, cols] = m1
+        v_out[own, cols] = v1
+        own_fold[b] = fold_rows(jnp.abs(w1))
+
+    def spread(scale):
+        return jnp.broadcast_to(scale, (16, TILE))
+
+    def recip(scale):
+        return spread(1.0 / (scale + SCALE_EPS))
+
+    def put(ref, value):
+        for b in range(BLOCKS):
+            ref[b] = value[b : b + 1]
+
+    own_max = widest(own_fold)
+    put(own_scale, spread(own_max))
+    put(own_recip, recip(own_max))
+
+    def target(k):
+        return (up(x + lax.div(k, 4), 4), up(y + lax.rem(k, 4), 4), half, z)
+
+    def bulk_start(k, rows, count):
+        pltpu.make_async_remote_copy(
+            src_ref=send.at[k, pl.ds(rows, count), :],
+            dst_ref=served.at[slot, pl.ds(rows, count), :],
+            send_sem=bulk_send,
+            recv_sem=bulk_recv,
+            device_id=target(k),
+            device_id_type=MESH,
+        ).start()
+
+    def bulk_home(rows, count):
+        @pl.when(is_self)
+        def _():
+            served[slot, pl.ds(rows, count), :] = send[0, pl.ds(rows, count), :]
+
+        @pl.when(jnp.logical_not(is_self))
+        def _():
+            bulk_start(0, rows, count)
+
+    @pl.loop(0, 16)
+    def _(k):
+        b = inverse[k]
+        send[k, own, :] = (w_blocks[b, own, :] * own_recip[b]).astype(bf16)
+
+    pl.semaphore_wait(barrier, 2 * (GROUP - 1))
+
+    @pl.loop(1, GROUP)
+    def _(d):
+        pltpu.make_async_remote_copy(
+            src_ref=lrow_out.at[0],
+            dst_ref=lrow_in.at[place],
+            send_sem=lrow_send,
+            recv_sem=lrow_recv,
+            device_id=group_device(d),
+            device_id_type=MESH,
+        ).start()
+
+    near = [
+        pltpu.make_async_remote_copy(
+            src_ref=lflat,
+            dst_ref=lnear.at[way],
+            send_sem=near_send.at[way],
+            recv_sem=near_recv.at[way],
+            device_id=(x, y, c, up(z + step, 8)),
+            device_id_type=MESH,
         )
-        lfold_b[b : b + 1, :] = jnp.max(
-            jnp.where(lat_rows >= lat_edge, size, 0.0), axis=0, keepdims=True
-        )
-    real = iota2((16, 1), 0) < LBLOCKS
-    first_lane = LANE0 + lat_block * LBLOCKS
-    max_a = jnp.where(real, jnp.max(lfold_a[...], axis=1, keepdims=True), 0.0)
-    max_b = jnp.where(real, jnp.max(lfold_b[...], axis=1, keepdims=True), 0.0)
-    lrow = jnp.maximum(lanes_of(max_a, first_lane), lanes_of(max_b, first_lane + LBLOCKS))
-    lrow_out[0] = lrow
-
-    for copy in loads[4:16]:
+        for way, step in ((0, 1), (1, 7))
+    ]
+    for copy in near:
+        copy.start()
+
+    @pl.loop(1, 16)
+    def _(k):
+        bulk_start(k, local, TILE)
+
+    bulk_home(local, TILE)
+
+    for copy in loads[8:20]:
         copy.wait()
 
     @pl.loop(0, BLOCKS)
@@ -255,13 +356,8 @@
         next_fold[b] = after
         prev_fold[b] = before
 
-    def widest(fold):
-        return jnp.max(jnp.max(fold[...], axis=1), axis=1, keepdims=True)
-
     edge_out[0] = lanes_of(widest(next_fold), 0)
     edge_out[1] = lanes_of(widest(prev_fold), 0)
-
-    pl.semaphore_wait(barrier, LINKS + 31)
 
     def edge_copy(n, place):
         return pltpu.make_async_remote_copy(
@@ -277,95 +373,6 @@
     for copy in edges:
         copy.start()
 
-    def lrow_copy(n, device):
-        return pltpu.make_async_remote_copy(
-            src_ref=lrow_out.at[0],
-            dst_ref=lrow_in.at[n],
-            send_sem=lrow_send,
-            recv_sem=lrow_recv,
-            device_id=device,
-            device_id_type=MESH,
-        )
-
-    @pl.loop(1, 8)
-    def _(d):
-        lrow_copy(d - 1, (x, y, c, up(z + d, 8))).start()
-
-    @pl.loop(1, 6)
-    def _(d):
-        lrow_copy(d + 6, quad_device(inner_next, up(z + d, 8))).start()
-
-    @pl.loop(3, 8)
-    def _(d):
-        lrow_copy(d + 9, quad_device(inner_prev, up(z + d, 8))).start()
-
-    for copy in loads[16:]:
-        copy.wait()
-    own = pl.ds(local, TILE)
-
-    @pl.loop(0, BLOCKS)
-    def _(b):
-        cols = pl.ds(pl.multiple_of(b * TILE, TILE), TILE)
-        w1, m1, v1 = adamw(
-            w_in[own, cols], m_in[own, cols], v_in[own, cols], g_in[own, cols], num_scale, den_scale
-        )
-        w_out[own, cols] = w1
-        w_blocks[b, own, :] = w1
-        m_out[own, cols] = m1
-        v_out[own, cols] = v1
-        own_fold[b] = fold_rows(jnp.abs(w1))
-
-    def spread(scale):
-        return jnp.broadcast_to(scale, (16, TILE))
-
-    def recip(scale):
-        return spread(1.0 / (scale + SCALE_EPS))
-
-    def put(ref, value):
-        for b in range(BLOCKS):
-            ref[b] = value[b : b + 1]
-
-    own_max = widest(own_fold)
-    put(own_scale, spread(own_max))
-    put(own_recip, recip(own_max))
-
-    def target(k):
-        return (up(x + lax.div(k, 4), 4), up(y + lax.rem(k, 4), 4), half, z)
-
-    def bulk(k, rows, start):
-        src = send.at[k, pl.ds(rows, start[1]), :]
-        dst = served.at[slot, pl.ds(rows, start[1]), :]
-        return src, dst
-
-    def bulk_start(k, rows, count):
-        src = send.at[k, pl.ds(rows, count), :]
-        dst = served.at[slot, pl.ds(rows, count), :]
-        stays = jnp.logical_and(is_self, k == 0)
-
-        @pl.when(stays)
-        def _():
-            pltpu.make_async_copy(src, dst, self_sem).start()
-
-        @pl.when(jnp.logical_not(stays))
-        def _():
-            pltpu.make_async_remote_copy(
-                src_ref=src,
-                dst_ref=dst,
-                send_sem=bulk_send,
-                recv_sem=bulk_recv,
-                device_id=target(k),
-                device_id_type=MESH,
-            ).start()
-
-    @pl.loop(0, 16)
-    def _(k):
-        b = inverse[k]
-        send[k, own, :] = (w_blocks[b, own, :] * own_recip[b]).astype(bf16)
-
-    @pl.loop(0, 16)
-    def _(k):
-        bulk_start(k, local, TILE)
-
     for copy in edges:
         copy.wait_recv()
     prev_max = blocks_of(jnp.maximum(edge_out[1], edge_in[0]), 0)
@@ -384,15 +391,9 @@
             scale = jnp.where(inner + j < 7, after, before)
             send[k, rows, :] = (w_blocks[b, rows, :] * scale).astype(bf16)
 
-    pltpu.make_async_copy(lrow_in, lrow_in, lrow_recv).wait()
-    lmax = jnp.maximum(lrow, jnp.max(lrow_in[...], axis=0))
-    lrecip_a[...] = recip(blocks_of(lmax, first_lane))
-    lrecip_b[...] = recip(blocks_of(lmax, first_lane + LBLOCKS))
-
-    for b in range(LBLOCKS):
-        cols = pl.ds(b * TILE, TILE)
-        scale = jnp.where(lat_rows < lat_edge, lrecip_a[b : b + 1, :], lrecip_b[b : b + 1, :])
-        lat[z, :, cols] = (lw_out[:, cols] * scale).astype(bf16)
+    few_rows = lrow_in.at[pl.ds(0, GROUP - 1)]
+    pltpu.make_async_copy(few_rows, few_rows, lrow_recv).wait()
+    lmax = jnp.max(lrow_in[...], axis=0)
 
     lane = iota2((1, TILE), 1)
     scale_lane = 7 * lax.div(slot, 4) + 2 * inner
@@ -407,40 +408,6 @@
     @pl.loop(0, 16)
     def _(k):
         rows_out[k] = message(k)
-
-    def ring_copy(way, hop, part):
-        origin = up(z + 8 - hop, 8) if way == 0 else up(z + hop, 8)
-        peer = up(z + 1, 8) if way == 0 else up(z + 7, 8)
-        view = lat.at[origin, :, pl.ds(part * HALF, HALF)]
-        n = (way * 4 + hop) * 2 + part
-        return pltpu.make_async_remote_copy(
-            src_ref=view,
-            dst_ref=view,
-            send_sem=ring_send.at[n],
-            recv_sem=ring_recv.at[n],
-            device_id=(x, y, c, peer),
-            device_id_type=MESH,
-        )
-
-    def arrived(way, hop, part):
-        origin = up(z + 7 - hop, 8) if way == 0 else up(z + 1 + hop, 8)
-        view = lat.at[origin, :, pl.ds(part * HALF, HALF)]
-        n = (way * 4 + hop) * 2 + part
-        pltpu.make_async_copy(view, view, ring_recv.at[n]).wait()
-
-    hops = [
-        (way, hop, part)
-        for hop in range(4)
-        for part in range(2)
-        for way in range(2)
-        if hop < 3 or part == way
-    ]
-    sent = []
-    for way, hop, part in hops:
-        if hop == 0:
-            copy = ring_copy(way, hop, part)
-            copy.start()
-            sent.append(copy)
 
     def rows_copy(k, core):
         return pltpu.make_async_remote_copy(
@@ -460,33 +427,86 @@
         rows_copy(k, 0).start()
         rows_copy(k, 1).start()
 
+
+    def lat_scale(src, origin):
+        lane_a, in_a = lat_blocks(origin)
+        scale_a = recip(blocks_of(lmax, lane_a))
+        scale_b = recip(blocks_of(lmax, lane_a + LBLOCKS))
+        for b in range(LBLOCKS):
+            rows = slice(b * LROWS, (b + 1) * LROWS)
+            scale = jnp.where(in_a, scale_a[b : b + 1, :], scale_b[b : b + 1, :])
+            lscaled[rows, :] = src[rows, :] * scale
+        lat[origin] = lscaled[...].astype(bf16)
+
+    def ring_copy(way, hop, part):
+        origin = up(z + 8 - hop, 8) if way == 0 else up(z + hop, 8)
+        peer = up(z + 1, 8) if way == 0 else up(z + 7, 8)
+        view = lat.at[origin, pl.ds(part * PART, PART), :]
+        n = (way * 4 + hop) * PARTS + part
+        return pltpu.make_async_remote_copy(
+            src_ref=view,
+            dst_ref=view,
+            send_sem=ring_send.at[n],
+            recv_sem=ring_recv.at[n],
+            device_id=(x, y, c, peer),
+            device_id_type=MESH,
+        )
+
+    def arrived(way, hop, part):
+        origin = up(z + 7 - hop, 8) if way == 0 else up(z + 1 + hop, 8)
+        view = lat.at[origin, pl.ds(part * PART, PART), :]
+        n = (way * 4 + hop) * PARTS + part
+        pltpu.make_async_copy(view, view, ring_recv.at[n]).wait()
+
+    hops = [
+        (way, hop, part)
+        for hop in range(1, 4)
+        for part in range(PARTS)
+        for way in range(2)
+        if hop < 3 or part == way
+    ]
+    sent = []
+
+    def ring_start(way, hop, part):
+        copy = ring_copy(way, hop, part)
+        copy.start()
+        sent.append(copy)
+
+    for way, origin in ((0, up(z + 7, 8)), (1, up(z + 1, 8))):
+        near[way].wait_recv()
+        lat_scale(lnear.at[way], origin)
+        for part in range(PARTS):
+            ring_start(way, 1, part)
+
     for j, s in zip(range(4, 7), slabs):
 
-        @pl.loop(0, 16)
+        @pl.loop(1, 16)
         def _(k):
             bulk_start(k, s, SUB)
+
+        bulk_home(s, SUB)
+
+    lat_scale(lflat, z)
 
     for way, hop, part in hops:
         arrived(way, hop, part)
         if (way, hop + 1, part) in hops:
-            copy = ring_copy(way, hop + 1, part)
-            copy.start()
-            sent.append(copy)
+            ring_start(way, hop + 1, part)
 
     for copy in sent:
         copy.wait_send()
     for copy in edges:
         copy.wait_send()
-    pltpu.make_async_copy(lrow_in, lrow_in, lrow_send).wait()
+    for copy in near:
+        copy.wait_send()
+    pltpu.make_async_copy(few_rows, few_rows, lrow_send).wait()
     few = rows_all.at[pl.ds(0, 31)]
     pltpu.make_async_copy(few, few, rows_send).wait()
     pltpu.make_async_copy(few, few, rows_recv).wait()
 
     @pl.when(is_self)
     def _():
-        one = served.at[0]
         rest = served.at[pl.ds(0, 15)]
-        pltpu.make_async_copy(one, one, self_sem).wait()
         pltpu.make_async_copy(rest, rest, bulk_send).wait()
         pltpu.make_async_copy(rest, rest, bulk_recv).wait()
 
@@ -517,6 +537,8 @@
     lserved_hbm,
     lscales_hbm,
     lserved,
+    ltall,
+    lflat,
     scales,
     lscales,
     lscales_tall,
@@ -540,7 +562,12 @@
     ):
         store(src, dst)
     for o in range(8):
-        lserved[o * LROWS : (o + 1) * LROWS, :] = lat_in[o]
+        lflat[...] = lat_in[o].astype(f32)
+        for b in range(LBLOCKS):
+            ltall[o * LROWS : (o + 1) * LROWS, b * TILE : (b + 1) * TILE] = lflat[
+                b * LROWS : (b + 1) * LROWS, :
+            ]
+    lserved[...] = ltall[...].astype(bf16)
     store(lserved, lserved_hbm)
     c = lax.axis_index("dp_2")
     mine = jnp.max(rows_in[pl.ds(c * 16, 16)], axis=0)
@@ -569,7 +596,6 @@
     step_count,
     column_owner,
 ):
-    smem = pl.BlockSpec(memory_space=pltpu.SMEM)
     hbm = pl.BlockSpec(memory_space=pltpu.HBM)
     vmem = pl.BlockSpec(memory_space=pltpu.VMEM)
     dma = pltpu.SemaphoreType.DMA
@@ -585,9 +611,9 @@
             pltpu.VMEM((LROWS, LCOLS), f32),
             pltpu.VMEM((LROWS, LCOLS), bf16),
             pltpu.VMEM((LROWS, LCOLS), bf16),
-            pltpu.VMEM((8, LROWS, LCOLS), bf16),
+            pltpu.VMEM((8, LFLAT, TILE), bf16),
         ),
-        in_specs=[smem, smem] + [hbm] * 8,
+        in_specs=[pl.BlockSpec(memory_space=pltpu.SMEM)] + [hbm] * 9,
         out_specs=(vmem,) * 9,
         scratch_shapes=[
             pltpu.VMEM((ROWS, COLS), f32),
@@ -610,37 +636,40 @@
             pltpu.VMEM((16, *row), f32),
             pltpu.VMEM((16, TILE), f32),
             pltpu.VMEM((16, TILE), f32),
-            pltpu.VMEM((16, TILE), f32),
-            pltpu.VMEM((16, TILE), f32),
             pltpu.VMEM((1, *row), f32),
-            pltpu.VMEM((LINKS, *row), f32),
+            pltpu.VMEM((GROUP, *row), f32),
             pltpu.VMEM((2, *row), f32),
             pltpu.VMEM((2, *row), f32),
             pltpu.VMEM((16, *row), f32),
+            pltpu.VMEM((LFLAT, TILE), f32),
+            pltpu.VMEM((LFLAT, TILE), f32),
+            pltpu.VMEM((2, LFLAT, TILE), f32),
             pltpu.SMEM((16,), jnp.int32),
-            dma((20,)),
-            dma,
+            pltpu.SMEM((16,), jnp.int32),
+            dma((21,)),
             dma,
             dma,
             dma,
             dma,
             dma((2,)),
             dma((2,)),
+            dma((2,)),
+            dma((2,)),
             dma,
             dma,
-            dma((16,)),
-            dma((16,)),
+            dma((8 * PARTS,)),
+            dma((8 * PARTS,)),
         ],
         compiler_params=pltpu.CompilerParams(
             collective_id=0, has_side_effects=True, vmem_limit_bytes=24 << 20
         ),
         name="step",
     )(
-        column_owner,
-        step_count,
+        pltpu.with_memory_space_constraint(step_count, pltpu.SMEM),
         *(
             pltpu.with_memory_space_constraint(value, pltpu.HBM)
             for value in (
+                column_owner,
                 expert_master[0],
                 expert_first[0],
                 expert_second[0],
@@ -670,6 +699,8 @@
         out_specs=(hbm,) * 10,
         scratch_shapes=[
             pltpu.VMEM((ROWS, LCOLS), bf16),
+            pltpu.VMEM((ROWS, LCOLS), f32),
+            pltpu.VMEM((LFLAT, TILE), f32),
             pltpu.VMEM((1, 28), f32),
             pltpu.VMEM((LBLOCKS, 56), f32),
             pltpu.VMEM((TILE, TILE), f32),

time: 35 us -> 32.6 us (0.931)
  the two profiles are of different devices: /device:TPU:8 before, /device:TPU:1 now
where the time goes in v2:
time: 32.6 us; the launch traced here: 32.3 us
  Pallas kernels  31 us (95%)
  between operations  1.3 us (4%)
    pallas_call x1, Pallas kernels, body(): pl.pallas_call(step_kernel, out_shape=(pltpu.VMEM((ROWS, COLS), f32), plt...  28.3 us
    pallas_call x1, Pallas kernels, body(): pl.pallas_call(store_kernel, out_shape=(jax.ShapeDtypeStruct((ROWS, COLS)...  2.64 us

profile of v2, /device:TPU:1, one launch (start us, length us, event | category | flops | bytes accessed | tf_op | source)
XLA Modules:
  0.0 32.3 jit_solution(17620686360977363231)
XLA Ops:
  1.3 28.3 %step.1 = (f32[224,2048]{1,0:T(8,128)S(1)}, bf16[224,2048]{1,0:T(8,128)(2,1)S(1)}, bf16[224,2048]{1,0:T(8,128)(2,1)S(1)}, bf16[16,224,128]{2,1,0:T(8,128)(2,1)S(...) custom-call(s32[1]{0:T(128)S(6)} %copy.20.step_count, ...), custom_call_target="tpu_custom_call" | custom-call | tf_op jit(solution)/shard_map/step/pallas_call | solution.py:603
  29.6 2.6 %store.1 = (f32[224,2048]{1,0:T(8,128)}, bf16[224,2048]{1,0:T(8,128)(2,1)}, bf16[224,2048]{1,0:T(8,128)(2,1)}, bf16[16,224,128]{2,1,0:T(8,128)(2,1)}, f32[1,28]{...) custom-call(f32[224,2048]{1,0:T(8,128)S(1)} %get-tuple-element.29.w_, ...), custom_call_target="tpu_custom_call" | custom-call | tf_op jit(solution)/shard_map/store/pallas_call | solution.py:684

commit v3 on v2

--- a/solution.py
+++ b/solution.py
@@ -28,7 +28,6 @@
 LFLAT = LROWS * LBLOCKS
 PARTS = 2
 PART = LFLAT // PARTS
-LANE0 = 32
 GROUP = 32
 
 f32 = jnp.float32
@@ -84,6 +83,7 @@
     v_out,
     served,
     rows_all,
+    groups_all,
     lw_out,
     lm_out,
     lv_out,
@@ -113,6 +113,7 @@
     edge_out,
     edge_in,
     rows_out,
+    groups_out,
     lflat,
     lscaled,
     lnear,
@@ -129,6 +130,8 @@
     near_recv,
     rows_send,
     rows_recv,
+    groups_send,
+    groups_recv,
     ring_send,
     ring_recv,
 ):
@@ -143,23 +146,39 @@
     slot = lax.rem(dp, 16)
     is_self = c == half
 
-    def dp_device(target, target_z):
-        return (lax.div(target, 8), lax.rem(lax.div(target, 2), 4), lax.rem(target, 2), target_z)
-
-    def quad_device(place, target_z):
-        return (x, quad + lax.div(place, 2), lax.rem(place, 2), target_z)
+    xs = [lax.rem(x + d, 4) for d in range(4)]
+    ys = [lax.rem(y + d, 4) for d in range(4)]
+    zs = [lax.rem(z + d, 8) for d in range(8)]
+    cs = [c, 1 - c]
+    quads = [lax.rem(inner + d, 4) for d in range(4)]
+    quads = [(quad + lax.div(n, 2), lax.rem(n, 2)) for n in quads]
+    place = inner * 8 + z
 
     def up(value, n):
         return lax.rem(value, n)
 
-    place = inner * 8 + z
-
-    def group_device(d):
-        other = up(place + d, GROUP)
-        return quad_device(lax.div(other, 8), up(other, 8))
-
-    inner_next = up(inner + 1, 4)
-    inner_prev = up(inner + 3, 4)
+    def far(d, n):
+        return min(d, n - d)
+
+    def target(k):
+        return (xs[k // 4], ys[k % 4], half, z)
+
+    group_devices = sorted(
+        ((di, dz) for di in range(4) for dz in range(8) if di or dz), key=lambda d: -far(d[1], 8)
+    )
+    group_devices = [(x, *quads[di], zs[dz]) for di, dz in group_devices]
+    near_y = 1 - 2 * lax.rem(y, 2)
+    plane_devices = [
+        (xs[dx], lax.rem(y + 4 + near_y * dy, 4), cs[dc], z)
+        for dx in (2, 1, 3, 0)
+        for dy in (2, 3, 1, 0)
+        for dc in range(2)
+        if dx or dy > 1
+    ]
+
+    barrier = pltpu.get_barrier_semaphore()
+    for device in group_devices + plane_devices:
+        pl.semaphore_signal(barrier, inc=1, device_id=device, device_id_type=MESH)
 
     loads = []
 
@@ -181,16 +200,6 @@
 
     load(owner_hbm, owner)
 
-    barrier = pltpu.get_barrier_semaphore()
-
-    def greet(device):
-        pl.semaphore_signal(barrier, inc=1, device_id=device, device_id_type=MESH)
-
-    @pl.loop(1, GROUP)
-    def _(d):
-        greet(group_device(d))
-        greet(dp_device(up(dp + d, GROUP), z))
-
     steps = jnp.full((8, TILE), step_count[0], jnp.int32).astype(f32)
     num_scale = (LEARN_RATE / (1.0 - jnp.power(jnp.full((8, TILE), BETA_ONE, f32), steps)))[0:1]
     den_scale = (1.0 / (1.0 - jnp.power(jnp.full((8, TILE), BETA_TWO, f32), steps)))[0:1]
@@ -201,7 +210,7 @@
 
     def lat_blocks(origin):
         start = (inner * 8 + origin) * LROWS
-        return LANE0 + lax.div(start, TILE) * LBLOCKS, lat_rows < TILE - lax.rem(start, TILE)
+        return lax.div(start, TILE) * LBLOCKS, lat_rows < TILE - lax.rem(start, TILE)
 
     first_lane, in_first = lat_blocks(z)
 
@@ -271,9 +280,6 @@
     put(own_scale, spread(own_max))
     put(own_recip, recip(own_max))
 
-    def target(k):
-        return (up(x + lax.div(k, 4), 4), up(y + lax.rem(k, 4), 4), half, z)
-
     def bulk_start(k, rows, count):
         pltpu.make_async_remote_copy(
             src_ref=send.at[k, pl.ds(rows, count), :],
@@ -298,16 +304,15 @@
         b = inverse[k]
         send[k, own, :] = (w_blocks[b, own, :] * own_recip[b]).astype(bf16)
 
-    pl.semaphore_wait(barrier, 2 * (GROUP - 1))
-
-    @pl.loop(1, GROUP)
-    def _(d):
+    pl.semaphore_wait(barrier, len(group_devices) + len(plane_devices))
+
+    for device in group_devices:
         pltpu.make_async_remote_copy(
             src_ref=lrow_out.at[0],
             dst_ref=lrow_in.at[place],
             send_sem=lrow_send,
             recv_sem=lrow_recv,
-            device_id=group_device(d),
+            device_id=device,
             device_id_type=MESH,
         ).start()
 
@@ -317,7 +322,7 @@
             dst_ref=lnear.at[way],
             send_sem=near_send.at[way],
             recv_sem=near_recv.at[way],
-            device_id=(x, y, c, up(z + step, 8)),
+            device_id=(x, y, c, zs[step]),
             device_id_type=MESH,
         )
         for way, step in ((0, 1), (1, 7))
@@ -325,11 +330,8 @@
     for copy in near:
         copy.start()
 
-    @pl.loop(1, 16)
-    def _(k):
+    for k in range(4, 16):
         bulk_start(k, local, TILE)
-
-    bulk_home(local, TILE)
 
     for copy in loads[8:20]:
         copy.wait()
@@ -359,19 +361,22 @@
     edge_out[0] = lanes_of(widest(next_fold), 0)
     edge_out[1] = lanes_of(widest(prev_fold), 0)
 
-    def edge_copy(n, place):
+    def edge_copy(n, step):
         return pltpu.make_async_remote_copy(
             src_ref=edge_out.at[n],
             dst_ref=edge_in.at[n],
             send_sem=edge_send.at[n],
             recv_sem=edge_recv.at[n],
-            device_id=quad_device(place, z),
+            device_id=(x, *quads[step], z),
             device_id_type=MESH,
         )
 
-    edges = [edge_copy(0, inner_next), edge_copy(1, inner_prev)]
+    edges = [edge_copy(0, 1), edge_copy(1, 3)]
     for copy in edges:
         copy.start()
+    for k in range(1, 4):
+        bulk_start(k, local, TILE)
+    bulk_home(local, TILE)
 
     for copy in edges:
         copy.wait_recv()
@@ -381,9 +386,15 @@
     put(next_recip, recip(next_max))
     put(next_scale, spread(next_max))
 
+    lane = iota2((1, TILE), 1)
+    scale_lane = 7 * lax.div(slot, 4) + 2 * inner
+    takes_next = jnp.logical_and(lane == scale_lane + 1, inner < 3)
+
     @pl.loop(0, 16)
     def _(k):
         b = inverse[k]
+        value = jnp.where(lane == scale_lane, own_scale[b], 0.0)
+        rows_out[k] = jnp.where(takes_next, next_scale[b], value)
         after = next_recip[b]
         before = prev_recip[b]
         for j, s in zip(range(4, 7), slabs):
@@ -391,42 +402,54 @@
             scale = jnp.where(inner + j < 7, after, before)
             send[k, rows, :] = (w_blocks[b, rows, :] * scale).astype(bf16)
 
+    def rows_start(k):
+        pltpu.make_async_remote_copy(
+            src_ref=rows_out.at[k],
+            dst_ref=rows_all.at[slot],
+            send_sem=rows_send,
+            recv_sem=rows_recv,
+            device_id=target(k),
+            device_id_type=MESH,
+        ).start()
+
+    for k in range(1, 16):
+        rows_start(k)
+
+    @pl.when(is_self)
+    def _():
+        rows_all[slot] = rows_out[0]
+
+    @pl.when(jnp.logical_not(is_self))
+    def _():
+        rows_start(0)
+
     few_rows = lrow_in.at[pl.ds(0, GROUP - 1)]
     pltpu.make_async_copy(few_rows, few_rows, lrow_recv).wait()
     lmax = jnp.max(lrow_in[...], axis=0)
-
-    lane = iota2((1, TILE), 1)
-    scale_lane = 7 * lax.div(slot, 4) + 2 * inner
-    lat_lanes = jnp.where(lane >= LANE0, lmax, 0.0)
-
-    def message(k):
-        b = inverse[k]
-        value = jnp.where(lane == scale_lane, own_scale[b], lat_lanes)
-        both = jnp.logical_and(lane == scale_lane + 1, inner < 3)
-        return jnp.where(both, next_scale[b], value)
-
-    @pl.loop(0, 16)
-    def _(k):
-        rows_out[k] = message(k)
-
-    def rows_copy(k, core):
-        return pltpu.make_async_remote_copy(
-            src_ref=rows_out.at[k],
-            dst_ref=rows_all.at[dp],
-            send_sem=rows_send,
-            recv_sem=rows_recv,
-            device_id=(up(x + lax.div(k, 4), 4), up(y + lax.rem(k, 4), 4), core, z),
+    group = 2 * x + lax.div(y, 2)
+    groups_out[0] = lmax
+    groups_all[group] = lmax
+
+    for dx, dy in [(dx, dy) for dx in range(4) for dy in (0, 2) if dx or dy]:
+        pltpu.make_async_remote_copy(
+            src_ref=groups_out.at[0],
+            dst_ref=groups_all.at[group],
+            send_sem=groups_send,
+            recv_sem=groups_recv,
+            device_id=(xs[dx], ys[dy], c, z),
             device_id_type=MESH,
-        )
-
-    rows_all[dp] = rows_out[0]
-    rows_copy(0, 1 - c).start()
-
-    @pl.loop(1, 16)
-    def _(k):
-        rows_copy(k, 0).start()
-        rows_copy(k, 1).start()
-
+        ).start()
+
+    def shared_start(n):
+        pieces = [(0, n * SUB), (n * SUB + TILE, ROWS - n * SUB - TILE)]
+
+        @pl.when(inner == n)
+        def _():
+            for rows, count in pieces:
+                if count:
+                    for k in range(1, 16):
+                        bulk_start(k, rows, count)
+                    bulk_home(rows, count)
 
     def lat_scale(src, origin):
         lane_a, in_a = lat_blocks(origin)
@@ -478,14 +501,8 @@
         for part in range(PARTS):
             ring_start(way, 1, part)
 
-    for j, s in zip(range(4, 7), slabs):
-
-        @pl.loop(1, 16)
-        def _(k):
-            bulk_start(k, s, SUB)
-
-        bulk_home(s, SUB)
-
+    for n in range(4):
+        shared_start(n)
     lat_scale(lflat, z)
 
     for way, hop, part in hops:
@@ -500,20 +517,25 @@
     for copy in near:
         copy.wait_send()
     pltpu.make_async_copy(few_rows, few_rows, lrow_send).wait()
-    few = rows_all.at[pl.ds(0, 31)]
-    pltpu.make_async_copy(few, few, rows_send).wait()
-    pltpu.make_async_copy(few, few, rows_recv).wait()
+    seven = groups_all.at[pl.ds(0, 7)]
+    pltpu.make_async_copy(seven, seven, groups_send).wait()
+    pltpu.make_async_copy(seven, seven, groups_recv).wait()
 
     @pl.when(is_self)
     def _():
         rest = served.at[pl.ds(0, 15)]
         pltpu.make_async_copy(rest, rest, bulk_send).wait()
         pltpu.make_async_copy(rest, rest, bulk_recv).wait()
+        rest = rows_all.at[pl.ds(0, 15)]
+        pltpu.make_async_copy(rest, rest, rows_send).wait()
+        pltpu.make_async_copy(rest, rest, rows_recv).wait()
 
     @pl.when(jnp.logical_not(is_self))
     def _():
         pltpu.make_async_copy(served, served, bulk_send).wait()
         pltpu.make_async_copy(served, served, bulk_recv).wait()
+        pltpu.make_async_copy(rows_all, rows_all, rows_send).wait()
+        pltpu.make_async_copy(rows_all, rows_all, rows_recv).wait()
 
 
 def store_kernel(
@@ -522,6 +544,7 @@
     v_in,
     served_in,
     rows_in,
+    groups_in,
     lw_in,
     lm_in,
     lv_in,
@@ -569,13 +592,11 @@
             ]
     lserved[...] = ltall[...].astype(bf16)
     store(lserved, lserved_hbm)
-    c = lax.axis_index("dp_2")
-    mine = jnp.max(rows_in[pl.ds(c * 16, 16)], axis=0)
-    scales[...] = mine[:, 0:28]
+    scales[...] = jnp.max(rows_in[...], axis=0)[:, 0:28]
     for g in range(8):
-        group = jnp.max(rows_in[4 * g : 4 * g + 4], axis=0)
+        group = groups_in[g]
         for r in range(7):
-            lane = LANE0 + r * LBLOCKS
+            lane = r * LBLOCKS
             lscales_tall[7 * g + r : 7 * g + r + 1, 0:LBLOCKS] = group[:, lane : lane + LBLOCKS]
     lscales[...] = lscales_tall[...].T[0:LBLOCKS, 0:56]
     store(scales, scales_hbm)
@@ -607,14 +628,15 @@
             pltpu.VMEM((ROWS, COLS), bf16),
             pltpu.VMEM((ROWS, COLS), bf16),
             pltpu.VMEM((16, ROWS, TILE), bf16),
-            pltpu.VMEM((32, *row), f32),
+            pltpu.VMEM((16, *row), f32),
+            pltpu.VMEM((8, *row), f32),
             pltpu.VMEM((LROWS, LCOLS), f32),
             pltpu.VMEM((LROWS, LCOLS), bf16),
             pltpu.VMEM((LROWS, LCOLS), bf16),
             pltpu.VMEM((8, LFLAT, TILE), bf16),
         ),
         in_specs=[pl.BlockSpec(memory_space=pltpu.SMEM)] + [hbm] * 9,
-        out_specs=(vmem,) * 9,
+        out_specs=(vmem,) * 10,
         scratch_shapes=[
             pltpu.VMEM((ROWS, COLS), f32),
             pltpu.VMEM((ROWS, COLS), bf16),
@@ -641,6 +663,7 @@
             pltpu.VMEM((2, *row), f32),
             pltpu.VMEM((2, *row), f32),
             pltpu.VMEM((16, *row), f32),
+            pltpu.VMEM((1, *row), f32),
             pltpu.VMEM((LFLAT, TILE), f32),
             pltpu.VMEM((LFLAT, TILE), f32),
             pltpu.VMEM((2, LFLAT, TILE), f32),
@@ -655,6 +678,8 @@
             dma((2,)),
             dma((2,)),
             dma((2,)),
+            dma,
+            dma,
             dma,
             dma,
             dma((8 * PARTS,)),
@@ -695,7 +720,7 @@
             jax.ShapeDtypeStruct((ROWS, LCOLS), bf16),
             jax.ShapeDtypeStruct((LBLOCKS, 56), f32),
         ),
-        in_specs=[vmem] * 9,
+        in_specs=[vmem] * 10,
         out_specs=(hbm,) * 10,
         scratch_shapes=[
             pltpu.VMEM((ROWS, LCOLS), bf16),

time: 32.6 us -> 30.8 us (0.945)
  Pallas kernels: 31 us -> 29.4 us
    pallas_call x1, Pallas kernels: 28.3 us -> 26.8 us  [body(): pl.pallas_call(step_kernel, out_shape=(pltpu.VMEM((ROWS, COLS), f32), plt...]
where the time goes in v3:
time: 30.8 us; the launch traced here: 30.7 us
  Pallas kernels  29.4 us (95%)
  between operations  1.3 us (4%)
    pallas_call x1, Pallas kernels, body(): pl.pallas_call(step_kernel, out_shape=(pltpu.VMEM((ROWS, COLS), f32), plt...  26.8 us
    pallas_call x1, Pallas kernels, body(): pl.pallas_call(store_kernel, out_shape=(jax.ShapeDtypeStruct((ROWS, COLS)...  2.58 us

profile of v3, /device:TPU:1, one launch (start us, length us, event | category | flops | bytes accessed | tf_op | source)
XLA Modules:
  0.0 30.7 jit_solution(16268162002749765304)
XLA Ops:
  1.3 26.8 %step.1 = (f32[224,2048]{1,0:T(8,128)S(1)}, bf16[224,2048]{1,0:T(8,128)(2,1)S(1)}, bf16[224,2048]{1,0:T(8,128)(2,1)S(1)}, bf16[16,224,128]{2,1,0:T(8,128)(2,1)S(...) custom-call(s32[1]{0:T(128)S(6)} %copy.20.step_count, ...), custom_call_target="tpu_custom_call" | custom-call | tf_op jit(solution)/shard_map/step/pallas_call | solution.py:624
  28.1 2.6 %store.1 = (f32[224,2048]{1,0:T(8,128)}, bf16[224,2048]{1,0:T(8,128)(2,1)}, bf16[224,2048]{1,0:T(8,128)(2,1)}, bf16[16,224,128]{2,1,0:T(8,128)(2,1)}, f32[1,28]{...) custom-call(f32[224,2048]{1,0:T(8,128)S(1)} %get-tuple-element.30.w_, ...), custom_call_target="tpu_custom_call" | custom-call | tf_op jit(solution)/shard_map/store/pallas_call | solution.py:709

commit v4 on v3

--- a/solution.py
+++ b/solution.py
@@ -7,6 +7,7 @@
 from jax.sharding import PartitionSpec as P
 
 MESH = pl.DeviceIdType.MESH
+SPREAD = (8, 4, 12, 9, 5, 13, 10, 6, 14, 11, 7, 15, 2, 1, 3)
 TILE = 128
 DP = ("dp_0", "dp_1", "dp_2")
 DP_EXPERT = ("dp_0", "dp_1", "dp_2", "expert")
@@ -330,7 +331,7 @@
     for copy in near:
         copy.start()
 
-    for k in range(4, 16):
+    for k in SPREAD[:12]:
         bulk_start(k, local, TILE)
 
     for copy in loads[8:20]:
@@ -374,7 +375,7 @@
     edges = [edge_copy(0, 1), edge_copy(1, 3)]
     for copy in edges:
         copy.start()
-    for k in range(1, 4):
+    for k in SPREAD[12:]:
         bulk_start(k, local, TILE)
     bulk_home(local, TILE)
 
@@ -447,7 +448,7 @@
         def _():
             for rows, count in pieces:
                 if count:
-                    for k in range(1, 16):
+                    for k in SPREAD:
                         bulk_start(k, rows, count)
                     bulk_home(rows, count)
 

time: 30.8 us -> 30.6 us (level)
  Pallas kernels: 29.4 us -> 29 us
    pallas_call x1, Pallas kernels: 26.8 us -> 26.4 us  [body(): pl.pallas_call(step_kernel, out_shape=(pltpu.VMEM((ROWS, COLS), f32), plt...]
where the time goes in v4:
time: 30.6 us; the launch traced here: 30.3 us
  Pallas kernels  29 us (95%)
  between operations  1.3 us (4%)
    pallas_call x1, Pallas kernels, body(): pl.pallas_call(step_kernel, out_shape=(pltpu.VMEM((ROWS, COLS), f32), plt...  26.4 us
    pallas_call x1, Pallas kernels, body(): pl.pallas_call(store_kernel, out_shape=(jax.ShapeDtypeStruct((ROWS, COLS)...  2.58 us

profile of v4, /device:TPU:1, one launch (start us, length us, event | category | flops | bytes accessed | tf_op | source)
XLA Modules:
  0.0 30.3 jit_solution(17152258671244247410)
XLA Ops:
  1.3 26.4 %step.1 = (f32[224,2048]{1,0:T(8,128)S(1)}, bf16[224,2048]{1,0:T(8,128)(2,1)S(1)}, bf16[224,2048]{1,0:T(8,128)(2,1)S(1)}, bf16[16,224,128]{2,1,0:T(8,128)(2,1)S(...) custom-call(s32[1]{0:T(128)S(6)} %copy.20.step_count, ...), custom_call_target="tpu_custom_call" | custom-call | tf_op jit(solution)/shard_map/step/pallas_call | solution.py:625
  27.7 2.6 %store.1 = (f32[224,2048]{1,0:T(8,128)}, bf16[224,2048]{1,0:T(8,128)(2,1)}, bf16[224,2048]{1,0:T(8,128)(2,1)}, bf16[16,224,128]{2,1,0:T(8,128)(2,1)}, f32[1,28]{...) custom-call(f32[224,2048]{1,0:T(8,128)S(1)} %get-tuple-element.30.w_, ...), custom_call_target="tpu_custom_call" | custom-call | tf_op jit(solution)/shard_map/store/pallas_call | solution.py:710
